TPU v7x, 32 devices: a whole 2x2x4 slice. The times are simulated.
32 devices in a mesh: groups: 2 (over y), seq: 4 (over x, core), heads: 4 (over z).
Axes of the slice: x: 2, y: 2, z: 4, core: 2. Of those that a mesh axis runs over, the one named last changes fastest.
Arguments:
- tokens: bfloat16 [4096, 8192], P(('groups', 'seq'), 'heads'), parts along dimension 0, may hold values from -6 to 6
- xz_weight: bfloat16 [8192, 32768], P(None, ('heads', 'seq')), may hold values from -0.0625 to 0.0625
- bc_weight: bfloat16 [8192, 2048], P(None, 'heads'), may hold values from -0.0625 to 0.0625
- step_weight: bfloat16 [8192, 256], P(None, 'heads'), may hold values from -0.0625 to 0.0625
- step_bias: float32 [256], P('heads'), may hold values from -4 to -2
- decay_log: float32 [256], P('heads'), may hold values from -5.3 to -0.7
- skip_gain: float32 [256], P('heads'), may hold values from 0.5 to 2
- conv_weight: float32 [4, 16384], P(None, 'heads'), may hold values from -3 to 3
- conv_bias: float32 [16384], P('heads'), may hold values from -3 to 3
- bc_conv_weight: float32 [4, 2048], replicated, may hold values from -3 to 3
- bc_conv_bias: float32 [2048], replicated, may hold values from -3 to 3
- norm_gain: float32 [16384], P('heads'), may hold values from 0.1 to 1.9
- step_bounds: int32 [32], P('groups'), parts along dimension 0, may hold values from 0 to 2047, as said below
- readers: int32 [32], P('groups'), parts along dimension 0, may hold values from 0 to 3, as said below
Outputs:
- mixed: bfloat16 [4096, 16384], P(('groups', 'seq'), 'heads'), parts along dimension 0
- handoff: bfloat16 [8, 4, 256, 64, 128], P(('groups', 'heads'), None, 'seq'), parts along dimension 0
There are 2 independent parts, one for each index of `groups`. A program takes and returns all parts, laid end to end along the dimension named above; an argument that names none is the same for every part. Nothing has to cross between parts.
Inputs may be any that keep to these rules, and one draw needn't show every extreme that they name: `step_bounds`: boundary j * 4 + i, for i < 4, lies in section j: positions j * 512 to (j + 1) * 512 - 1. The first boundary is at position 0 and the last at 2047. `readers`: among the 4 boundaries of each section every reader appears exactly once.
All inputs are finite; a program needn't handle non-finite values.
Results may differ from a plain program's by a relative error of at most 0.0056.
Values may be sent and summed in bfloat16 or wider, within the bound.
A program may use at most 384 MiB of HBM per device.

v0:
```python
import jax
import jax.numpy as jnp
from jax import lax
from jax.sharding import PartitionSpec as P

H = 256
P_SIZE = 64
N = 128
G = 8
CH = 256
EPSILON = 1e-05
HIGHEST_PRECISION = lax.Precision.HIGHEST


def from_behind(value, axis, steps):
    count = lax.axis_size(axis)
    first, last = (max(0, -steps), min(count, count - steps))
    return lax.ppermute(value, axis, [(source, source + steps) for source in range(first, last)])


def entering(part, axis, combine, identity):
    place = lax.axis_index(axis)
    gathered = jax.tree.map(lambda a: lax.all_gather(a, axis), part)
    state = jax.tree.map(lambda a, e: jnp.zeros_like(a) + jnp.asarray(e, a.dtype), part, identity)

    def one(step, state):
        return combine(
            state, jax.tree.map(lambda a: lax.dynamic_index_in_dim(a, step, 0, False), gathered)
        )

    return lax.fori_loop(0, place, one, state)


def conv_rows(prefix, raw_rows, kernel, shift_bias):
    row_count = raw_rows.shape[0]
    padded = jnp.concatenate([prefix, raw_rows], axis=0).astype(jnp.float32)
    summed = jnp.broadcast_to(shift_bias[None, :], raw_rows.shape)
    for tap_index in range(kernel.shape[0]):
        summed = summed + kernel[tap_index][None, :] * padded[tap_index : tap_index + row_count]
    return jax.nn.silu(summed).astype(jnp.bfloat16)


def shards(
    tokens,
    xz_weight,
    bc_weight,
    step_weight,
    step_bias,
    decay_log,
    skip_gain,
    conv_weight,
    conv_bias,
    bc_conv_weight,
    bc_conv_bias,
    norm_gain,
    step_bounds,
    readers,
):
    head_devices = lax.axis_size("heads")
    section = lax.axis_index("seq")
    head_block = lax.axis_index("heads")
    local_heads = H // head_devices
    per_group = H // G
    local_groups = max(1, local_heads // per_group)
    group_heads = local_heads // local_groups
    first_group = head_block * local_heads // per_group
    gathered = lax.all_gather(tokens, "heads", axis=1, tiled=True)
    row_count = gathered.shape[0]
    xz_rows = jnp.dot(
        gathered,
        lax.all_gather(xz_weight, "seq", axis=1, tiled=True),
        preferred_element_type=jnp.float32,
    ).astype(jnp.bfloat16)
    head_cols = xz_rows.reshape(row_count, local_heads, 2 * P_SIZE)
    inner_raw = head_cols[:, :, :P_SIZE].reshape(row_count, local_heads * P_SIZE)
    gate_raw = head_cols[:, :, P_SIZE:].reshape(row_count, local_groups, group_heads, P_SIZE)
    bc_part = jnp.dot(gathered, bc_weight, preferred_element_type=jnp.float32).astype(jnp.bfloat16)
    step_raw = jnp.dot(gathered, step_weight, preferred_element_type=jnp.float32)
    bc_every = lax.all_gather(bc_part, "heads", axis=1, tiled=True)
    width_bc = local_groups * 2 * N
    bc_mine = lax.dynamic_slice_in_dim(bc_every, first_group * 2 * N, width_bc, 1)
    kernel_bc = lax.dynamic_slice_in_dim(bc_conv_weight, first_group * 2 * N, width_bc, 1)
    shift_bc = lax.dynamic_slice_in_dim(bc_conv_bias, first_group * 2 * N, width_bc, 0)
    taps = conv_weight.shape[0]
    joined = jnp.concatenate([inner_raw, bc_mine], axis=1)
    previous = from_behind(joined[row_count - taps + 1 :], "seq", 1)
    inner_conv = conv_rows(
        previous[:, : local_heads * P_SIZE], inner_raw, conv_weight, conv_bias
    ).reshape(row_count, local_groups, group_heads, P_SIZE)
    bc_conv = conv_rows(previous[:, local_heads * P_SIZE :], bc_mine, kernel_bc, shift_bc).reshape(
        row_count, local_groups, 2 * N
    )
    b_input = bc_conv[:, :, :N]
    c_input = bc_conv[:, :, N:]
    step_size = jax.nn.softplus(step_raw + step_bias[None, :]).reshape(
        row_count, local_groups, group_heads
    )
    decay_rate = -jnp.exp(decay_log).reshape(local_groups, group_heads)[None] * step_size
    blocks = row_count // CH
    causal = lax.broadcasted_iota(jnp.int32, (CH, CH), 0) >= lax.broadcasted_iota(
        jnp.int32, (CH, CH), 1
    )
    running = jnp.zeros((local_groups, group_heads, P_SIZE, N), jnp.float32)
    local_starts = []
    intra_parts = []
    cum_parts = []
    block_totals = []
    for block_index in range(blocks):
        first_row = block_index * CH
        inner_blk = inner_conv[first_row : first_row + CH]
        b_blk = b_input[first_row : first_row + CH]
        c_blk = c_input[first_row : first_row + CH]
        step_blk = step_size[first_row : first_row + CH]
        cum_block = jnp.cumsum(decay_rate[first_row : first_row + CH], axis=0)
        scores = jnp.einsum("tgn,sgn->gts", c_blk, b_blk, preferred_element_type=jnp.float32)
        cum_gap = cum_block[:, None] - cum_block[None, :]
        weight = (
            jnp.where(causal[:, :, None, None], jnp.exp(jnp.minimum(cum_gap, 0.0)), 0.0)
            * step_blk[None]
        )
        mixing = (weight * jnp.transpose(scores, (1, 2, 0))[:, :, :, None]).astype(jnp.bfloat16)
        intra_parts.append(
            jnp.einsum("tsgr,sgrp->tgrp", mixing, inner_blk, preferred_element_type=jnp.float32)
        )
        cum_parts.append(cum_block)
        local_starts.append(running)
        block_total = cum_block[-1]
        block_totals.append(block_total)
        carry_weight = jnp.exp(block_total[None] - cum_block) * step_blk
        weighted = (inner_blk.astype(jnp.float32) * carry_weight[..., None]).astype(jnp.bfloat16)
        running = jnp.exp(block_total)[..., None, None] * running + jnp.einsum(
            "sgrp,sgn->grpn", weighted, b_blk, preferred_element_type=jnp.float32
        )
    section_decay = block_totals[0]
    block_index = 1
    section_decay = section_decay + block_totals[block_index]

    def combine(earlier, later):
        return (earlier[0] + later[0], jnp.exp(later[0])[..., None, None] * earlier[1] + later[1])

    identity = (jnp.zeros_like(section_decay), jnp.zeros_like(running))
    incoming = entering((section_decay, running), "seq", combine, identity)[1]
    global_starts = []
    ssd_parts = []
    prior_decay = jnp.zeros_like(section_decay)
    for block_index in range(blocks):
        start_state = local_starts[block_index] + jnp.exp(prior_decay)[..., None, None] * incoming
        global_starts.append(start_state)
        prior_decay = prior_decay + block_totals[block_index]
        first_row = block_index * CH
        c_blk = c_input[first_row : first_row + CH]
        outer_part = jnp.exp(cum_parts[block_index])[..., None] * jnp.einsum(
            "tgn,grpn->tgrp", c_blk.astype(jnp.float32), start_state, precision=HIGHEST_PRECISION
        )
        ssd_parts.append(intra_parts[block_index] + outer_part)
    ssd = jnp.concatenate(ssd_parts, axis=0) + skip_gain.reshape(local_groups, group_heads)[
        None, :, :, None
    ] * inner_conv.astype(jnp.float32)
    gated = ssd * jax.nn.silu(gate_raw.astype(jnp.float32))
    local_square = jnp.sum(gated * gated, axis=(2, 3))
    placed = lax.dynamic_update_slice_in_dim(
        jnp.zeros((row_count, G), jnp.float32), local_square, first_group, 1
    )
    square_total = lax.psum(placed, "heads")
    square_mean = lax.dynamic_slice_in_dim(square_total, first_group, local_groups, 1) / (
        per_group * P_SIZE
    )
    normed = (
        gated
        * lax.rsqrt(square_mean + EPSILON)[:, :, None, None]
        * norm_gain.reshape(local_groups, group_heads, P_SIZE)[None]
    )
    mixed = normed.astype(jnp.bfloat16).reshape(row_count, local_heads * P_SIZE)
    cum_all = jnp.concatenate(cum_parts, axis=0)
    starts_all = jnp.stack(global_starts, axis=0)
    positions = lax.broadcasted_iota(jnp.int32, (row_count,), 0)
    bound_local = (
        lax.dynamic_slice_in_dim(step_bounds, section * head_devices, head_devices, 0)
        - section * row_count
    )
    reader_local = lax.dynamic_slice_in_dim(readers, section * head_devices, head_devices, 0)
    block_of = bound_local // CH
    cum_at = cum_all[bound_local]
    inside_mask = (positions[None, :] // CH == block_of[:, None]) & (
        positions[None, :] <= bound_local[:, None]
    )
    cum_gap = cum_at[:, None] - cum_all[None]
    bound_weight = (
        jnp.where(inside_mask[:, :, None, None], jnp.exp(jnp.minimum(cum_gap, 0.0)), 0.0)
        * step_size[None]
    )
    bound_weighted = (inner_conv[None].astype(jnp.float32) * bound_weight[..., None]).astype(
        jnp.bfloat16
    )
    inside = jnp.einsum(
        "bsgrp,sgn->bgrpn", bound_weighted, b_input, preferred_element_type=jnp.float32
    )
    states = jnp.exp(cum_at)[..., None, None] * starts_all[block_of] + inside
    inverse = jnp.argsort(reader_local)
    ordered = states[inverse].reshape(head_devices, local_heads, P_SIZE, N).astype(jnp.bfloat16)
    arrived = lax.all_to_all(
        lax.all_to_all(ordered, "heads", split_axis=0, concat_axis=1, tiled=True),
        "seq",
        split_axis=1,
        concat_axis=0,
        tiled=True,
    )
    return (mixed, arrived[None])


def solution(mesh):
    in_specs = (
        P(("groups", "seq"), "heads"),
        P(None, ("heads", "seq")),
        P(None, "heads"),
        P(None, "heads"),
        P("heads"),
        P("heads"),
        P("heads"),
        P(None, "heads"),
        P("heads"),
        P(),
        P(),
        P("heads"),
        P("groups"),
        P("groups"),
    )
    out_specs = (P(("groups", "seq"), "heads"), P(("groups", "heads"), None, "seq", None, None))
    return jax.shard_map(shards, mesh=mesh, in_specs=in_specs, out_specs=out_specs, check_vma=False)
```

profile of v0, /device:TPU:6, one launch (start us, length us, event | category | flops | bytes accessed | tf_op | source)
XLA Modules:
  0.0 1422.9 jit_solution(13541814008040680989)
XLA Ops:
  8.0 152.5 %all-gather.6.cloned.1.call-done = bf16[512,8192]{1,0:T(8,128)(2,1)} async-done(((bf16[512,2048]{1,0:T(8,128)(2,1)}), bf16[512,8192]{1,0:T(8,128)(2,1)}) %all-gather.6.cloned.1.call-update) | async-done | bytes 8388624 | tf_op jit(solution)/shard_map/all_gather | solution.py:67
  160.4 11.0 convolution_convert_fusion.1
  172.7 0.8 dynamic_slice.29
  173.5 0.9 constant_dynamic-slice_fusion
  174.6 6.4 compare_select_fusion
  181.1 1.2 reduce-window.16
  182.2 1.2 reduce-window.14
  184.3 0.7 fusion.62
  185.7 30.3 %all-gather.10.cloned.1.call-done = bf16[512,2048]{1,0:T(8,128)(2,1)} async-done(((bf16[512,512]{1,0:T(8,128)(2,1)}), bf16[512,2048]{1,0:T(8,128)(2,1)}) %all-gather.10.cloned.1.call-update) | async-done | bytes 2097168 | tf_op jit(solution)/shard_map/all_gather | solution.py:79
  215.9 1.1 constant_dynamic-slice_fusion.1
  217.0 773.3 %all-gather.8.cloned.1.call-done = bf16[8192,8192]{1,0:T(8,128)(2,1)} async-done(((bf16[8192,2048]{1,0:T(8,128)(2,1)}), bf16[8192,8192]{1,0:T(8,128)(2,1)}) %all-gather.8.cloned.1.call-update) | async-done | bytes 134217744 | tf_op jit(solution)/shard_map/all_gather | solution.py:71
  990.3 79.7 %convolution_convert_fusion = bf16[512,8192]{1,0:T(8,128)(2,1)} fusion(bf16[512,8192]{1,0:T(8,128)(2,1)} %all-gather.6.cloned.1.call-done, bf16[8192,8192]{1,0:T(8,128)(2,1)} %all-gather.8.cloned.1.call-done), kind=kOutput, calls=%fused_computation.11 | convolution fusion | flops 68723671040 | bytes 150994944 | tf_op jit(solution)/shard_map/dot_general | solution.py:69
  1070.1 12.0 copy.125
  1082.1 7.6 slice_convert_fusion
  1089.6 6.3 copy.101
  1095.9 0.9 pad_maximum_fusion.2
  1096.8 2.7 collective-permute-start
  1100.1 2.0 collective-permute-done
  1104.0 4.5 maximum_convert_fusion
  1108.6 10.7 multiply_convert_fusion.6
  1119.7 1.3 copy-done.5
  1120.9 0.7 fusion.33
  1121.7 1.3 copy-done.3
  1123.0 2.1 multiply_add_fusion.1
  1125.3 0.8 sort.17
  1127.3 5.1 all_gather.22
  1132.5 1.1 convolution_bitcast_fusion.1
  1133.6 1.0 convolution_bitcast_fusion
  1134.6 48.9 %all-gather.12.cloned.1.call-done = f32[8,32,64,128]{3,2,1,0:T(8,128)} async-done(((f32[2,32,64,128]{3,2,1,0:T(8,128)}), f32[8,32,64,128]{3,2,1,0:T(8,128)}) %all-gather.12.cloned.1.call-update) | async-done | bytes 8388624 | tf_op jit(solution)/shard_map/all_gather | solution.py:23
  1183.8 4.2 while.12
  1183.9 2.0 bitcast_add_fusion.3
  1185.9 2.0 bitcast_add_fusion.3
  1188.1 1.9 fusion.41
  1190.0 5.5 fusion.42
  1195.4 3.8 fusion.44
  1199.3 2.4 pad_maximum_fusion
  1201.6 6.8 gather_fusion.1
  1208.5 7.2 fusion.31
  1215.8 6.8 fusion.32
  1222.7 14.6 %fusion.15 = (f32[512,2]{0,1:T(2,128)S(1)}, f32[512,4096]{0,1:T(8,128)}) fusion(f32[256,2,32,64]{0,3,2,1:T(8,128)S(1)} %fusion.31, f32[256,2,32,64]{0,3,2,1:T(8,128)} %fusion.32, f32[512,2,32,64]{0,3,2,1:T(8,128)} %bitcast.150, f32[2,32]{1,0:T(2,128)S(1)} %mul.366, f32[515,4096]{0,1:T(8,128)S(1)} %bitcast.147, f32[4096]{0:T(1024)S(1)} %bitcast.176, ...), kind=kLoop, calls=%fused_computation.30 | loop fusion | flops 50330624 | bytes 58806528 | tf_op jit(solution)/shard_map/reduce_sum | solution.py:160
  1237.3 9.6 bitcast_add_fusion.1
  1247.0 5.3 gather_fusion.2
  1252.3 99.6 %all_to_all.24 = bf16[4,64,64,128]{3,2,1,0:T(8,128)(2,1)} all-to-all(bf16[4,64,64,128]{3,2,1,0:T(8,128)(2,1)} %bitcast.155), channel_id=1, replica_groups=mesh['groups'=2,'seq'=4,'heads'=4] {'heads'}, dimensions={0} | all-to-all | bytes 8388608 | tf_op jit(solution)/shard_map/all_to_all | solution.py:202
  1351.9 4.8 all-to-all-start.1
  1357.0 17.2 %psum.7 = f32[512,8]{0,1:T(8,128)S(1)} all-reduce(f32[512,8]{0,1:T(8,128)S(1)} %dynamic_update_slice.3), channel_id=1, replica_groups=mesh['groups'=2,'seq'=4,'heads'=4] {'heads'}, use_global_device_ids=true, to_apply=%region_7.8 | all-reduce | flops 4096 | bytes 32768 | tf_op jit(solution)/shard_map/psum | solution.py:164
  1374.3 30.4 %fusion.12 = bf16[512,4096]{0,1:T(8,128)(2,1)} fusion(f32[256,4096]{0,1:T(8,128)} %bitcast.156, f32[256,4096]{0,1:T(8,128)} %bitcast.157, f32[512,64,64]{0,2,1:T(8,128)} %get-tuple-element.76, f32[4096]{0:T(1024)S(1)} %copy-done.29, f32[512,2]{0,1:T(2,128)S(1)} %add_rsqrt_fusion, f32[4096]{0:T(1024)S(1)} %mul.368, f32[515,4096]{0,1:T(8,128)} %copy-done.2, ...), kind=kLoop, calls=%fused_computation.26 | loop fusion | flops 52428800 | bytes 54644736 | tf_op jit(solution)/shard_map/convert_element_type | solution.py:173
  1404.6 6.3 copy.119
  1411.0 5.2 copy.181
  (144 shorter events, 8.5 us)
Async XLA Ops:
  7.2 167.3 %copy-start = (bf16[8192,64]{0,1:T(8,128)(2,1)S(1)}, bf16[8192,64]{0,1:T(8,128)(2,1)}, u32[]{:S(2)}) copy-start(bf16[8192,64]{0,1:T(8,128)(2,1)} %param.19) | copy-start | bytes 3145732
  7.2 153.3 %all-gather.6.cloned.1.call-start = ((), (), s32[]{:S(2)}) async-start(), calls=%async_computation.2 | async-start | bytes 10485760 | tf_op jit(solution)/shard_map/all_gather | solution.py:67
  7.9 208.0 %all-gather.10.cloned.1.call-start = ((), (), s32[]{:S(2)}) async-start(), calls=%async_computation.4 | async-start | bytes 2621440 | tf_op jit(solution)/shard_map/all_gather | solution.py:79
  171.5 1.1 copy-start.33
  171.5 2.9 copy-start.24
  171.5 3.0 copy-start.31
  171.5 818.8 %all-gather.8.cloned.1.call-start = ((), (), s32[]{:S(2)}) async-start(), calls=%async_computation.3 | async-start | bytes 167772160 | tf_op jit(solution)/shard_map/all_gather | solution.py:71
  172.3 1011.3 %all-gather.12.cloned.1.call-start = ((), (), s32[]{:S(2)}) async-start(), calls=%async_computation.5 | async-start | bytes 10485760 | tf_op jit(solution)/shard_map/all_gather | solution.py:23
  174.5 934.0 %copy-start.16 = (f32[1,4096]{1,0:T(1,128)}, f32[1,4096]{1,0:T(1,128)S(1)}, u32[]{:S(2)}) copy-start(f32[1,4096]{1,0:T(1,128)S(1)} %get-tuple-element.96) | copy-start | bytes 49156
  174.5 934.0 %copy-start.18 = (f32[1,4096]{1,0:T(1,128)}, f32[1,4096]{1,0:T(1,128)S(1)}, u32[]{:S(2)}) copy-start(f32[1,4096]{1,0:T(1,128)S(1)} %get-tuple-element.97) | copy-start | bytes 49156
  174.5 934.0 %copy-start.20 = (f32[1,4096]{1,0:T(1,128)}, f32[1,4096]{1,0:T(1,128)S(1)}, u32[]{:S(2)}) copy-start(f32[1,4096]{1,0:T(1,128)S(1)} %get-tuple-element.98) | copy-start | bytes 49156
  184.2 885.8 %copy-start.12 = (f32[256,64]{0,1:T(8,128)}, f32[256,64]{0,1:T(8,128)S(1)}, u32[]{:S(2)}) copy-start(f32[256,64]{0,1:T(8,128)S(1)} %get-tuple-element.85) | copy-start | bytes 196612
  184.3 885.8 %copy-start.14 = (f32[256,64]{0,1:T(8,128)}, f32[256,64]{0,1:T(8,128)S(1)}, u32[]{:S(2)}) copy-start(f32[256,64]{0,1:T(8,128)S(1)} %get-tuple-element.84) | copy-start | bytes 196612
  1096.8 5.3 collective-permute-start
  1100.1 21.6 %copy-start.27 = (f32[2,32]{1,0:T(2,128)}, f32[2,32]{1,0:T(2,128)S(1)}, u32[]{:S(2)}) copy-start(f32[2,32]{1,0:T(2,128)S(1)} %get-tuple-element.104) | copy-start | bytes 772
  1103.1 29.5 %copy-start.10 = (bf16[512,2,256]{2,1,0:T(2,128)(2,1)}, bf16[512,2,256]{2,1,0:T(2,128)(2,1)S(1)}, u32[]{:S(2)}) copy-start(bf16[512,2,256]{2,1,0:T(2,128)(2,1)S(1)} %reshape.225) | copy-start | bytes 1572868
  1103.5 5.1 copy-start.22
  1108.5 10.8 copy-start.2
  1119.6 1.3 copy-start.5
  1119.6 2.1 copy-start.7
  1119.6 5.5 copy-start.34
  1119.6 5.6 copy-start.35
  1119.7 6.4 copy-start.32
  1121.7 1.3 copy-start.3
  1183.8 4.2 copy-start.28
  1183.8 4.2 copy-start.30
  1201.6 6.8 copy-start.8
  1201.6 6.8 copy-start.15
  1201.6 6.8 copy-start.26
  1208.5 7.2 copy-start.6
  1208.5 7.2 copy-start.9
  1208.5 7.2 copy-start.11
  1208.5 7.2 copy-start.13
  1208.5 7.2 copy-start.25
  1215.7 7.0 copy-start.4
  1215.7 7.0 slice-start
  1215.8 6.9 slice-start.1
  1215.8 6.9 slice-start.2
  1215.8 6.9 copy-start.17
  1215.8 6.9 copy-start.19
  1215.8 6.9 copy-start.21
  1215.8 6.9 copy-start.23
  1222.7 14.6 %slice-start.3 = ((bf16[512,2,256]{2,1,0:T(2,128)(2,1)}), bf16[512,2,128]{2,1,0:T(2,128)(2,1)S(1)}, s32[]{:S(2)}) async-start(bf16[512,2,256]{2,1,0:T(2,128)(2,1)} %copy-done.10), calls=%async_computation.9 | async-start | bytes 524288 | tf_op jit(solution)/shard_map/slice | solution.py:93
  1252.3 121.9 %copy-start.29 = (f32[4096]{0:T(1024)S(1)}, f32[4096]{0:T(1024)}, u32[]{:S(2)}) copy-start(f32[4096]{0:T(1024)} %param.27) | copy-start | bytes 49156
  1351.9 59.1 %all-to-all-start.1 = ((bf16[1,256,64,128]{3,2,0,1:T(8,128)(2,1)}), bf16[1,256,64,128]{3,2,0,1:T(8,128)(2,1)}, u32[]{:S(2)}, u32[]{:S(2)}) async-start(bf16[1,256,64,128]{3,2,0,1:T(8,128)(2,1)} %bitcast.154), calls=%async_computation.1 | async-start | bytes 8388608 | tf_op jit(solution)/shard_map/all_to_all | solution.py:201
  1374.2 41.9 %copy-start.1 = (bf16[8192,64]{0,1:T(8,128)(2,1)S(1)}, bf16[8192,64]{0,1:T(8,128)(2,1)}, u32[]{:S(2)}) copy-start(bf16[8192,64]{0,1:T(8,128)(2,1)} %param.19) | copy-start | bytes 3145732
Sparse Core Ops, SparseCore 0:
  9.6 150.8 all-gather.5
  171.6 44.2 all-gather.9
  217.5 772.7 all-gather.7
  1125.2 58.2 all-gather.11
where the time goes:
time: 1430 us; the launch traced here: 1420 us
  waiting for transfers between devices  1010 us (71%)
  matrix products  135 us (9%)
  blocking collectives  122 us (9%)
  other arithmetic  83.8 us (6%)
  local copies, waits for them, and re-layouts  50.9 us (4%)
  between operations  14.8 us (1%)
    all_gather x1, waiting for transfers between devices, shards(): lax.all_gather(xz_weight, 'seq', axis=1, tiled=True)  773 us
    all_gather x1, waiting for transfers between devices, shards(): gathered = lax.all_gather(tokens, 'heads', axis=1, tiled=True)  152 us
    all_to_all x1, blocking collectives, shards(): lax.all_to_all(ordered, 'heads', split_axis=0, concat_axis=1, tiled=True)  99.6 us
    dot_general x1, matrix products, shards(): jnp.dot(gathered, lax.all_gather(xz_weight, 'seq', axis=1, tiled=True), p...  79.7 us
    all_gather x1, waiting for transfers between devices, entering(): gathered = jax.tree.map(lambda a: lax.all_gather(a, axis), part)  48.9 us
    convert_element_type x1, other arithmetic, shards(): mixed = normed.astype(jnp.bfloat16).reshape(row_count, local_heads * P_SIZE)  30.4 us
    all_gather x1, waiting for transfers between devices, shards(): bc_every = lax.all_gather(bc_part, 'heads', axis=1, tiled=True)  30.3 us
  transfers between devices with their start and end apart: 6, of which 5 were waited for; matrix products, arithmetic and copies ran while one was open for 4% of the time, Pallas kernels for 0%

commit v1 on v0

--- a/solution.py
+++ b/solution.py
@@ -2,6 +2,7 @@
 import jax.numpy as jnp
 from jax import lax
 from jax.sharding import PartitionSpec as P
+from jax.lax import axis_index, axis_size, ppermute
 
 H = 256
 P_SIZE = 64
@@ -10,6 +11,35 @@
 CH = 256
 EPSILON = 1e-05
 HIGHEST_PRECISION = lax.Precision.HIGHEST
+
+
+def load_the_chains(array_in, axis_no):
+    array_in = jnp.moveaxis(array_in, 0, axis_no)
+    v_now = array_in.shape
+    return array_in.reshape(
+        *v_now[:axis_no], v_now[axis_no] * v_now[axis_no + 1], *v_now[axis_no + 2 :]
+    )
+
+
+def _extend_modes(axis_key, here_x, array_dim=1):
+    n_all = axis_size(axis_key)
+    a_next = range(n_all)
+    carry = map(lambda d: (d, (d + 1) % n_all), a_next)
+    buffers = list(carry)
+    found = [(idx, ix) for ix, idx in buffers]
+    everything, x_new = ([], [])
+    for tick in [*range(n_all - 1)]:
+        if tick % 2 == 0:
+            everything.append(ppermute(everything[-1] if everything else here_x, axis_key, buffers))
+        else:
+            latest = ppermute(x_new[-1] if x_new else here_x, axis_key, found)
+            x_new.append(latest)
+    arr_now = jnp.stack([*everything[::-1], here_x, *x_new], axis=0)
+    near = axis_index(axis_key)
+    front = len(everything)
+    local_now = near - front
+    arr_now = arr_now[(jnp.arange(n_all) - local_now) % n_all]
+    return load_the_chains(arr_now, array_dim)
 
 
 def from_behind(value, axis, steps):
@@ -67,9 +97,7 @@
     gathered = lax.all_gather(tokens, "heads", axis=1, tiled=True)
     row_count = gathered.shape[0]
     xz_rows = jnp.dot(
-        gathered,
-        lax.all_gather(xz_weight, "seq", axis=1, tiled=True),
-        preferred_element_type=jnp.float32,
+        gathered, _extend_modes("seq", xz_weight), preferred_element_type=jnp.float32
     ).astype(jnp.bfloat16)
     head_cols = xz_rows.reshape(row_count, local_heads, 2 * P_SIZE)
     inner_raw = head_cols[:, :, :P_SIZE].reshape(row_count, local_heads * P_SIZE)

time: 1430 us -> 2440 us (1.71)
  local copies, waits for them, and re-layouts: 50.9 us -> 866 us
  other arithmetic: 83.8 us -> 175 us
  waiting for transfers between devices: 1010 us -> 1100 us
    ppermute x0 -> x3, waiting for transfers between devices: none -> 874 us  [the longest x2 874 us: _extend_modes(): ppermute(everything[-1] if everything else here_x, axis_key, buffers)]
    all_gather x1 -> x0, waiting for transfers between devices: 773 us -> none  [shards(): lax.all_gather(xz_weight, 'seq', axis=1, tiled=True)]
    gather x0 -> x257, local copies, waits for them, and re-layouts: none -> 644 us
    unnamed x81 -> x161, local copies, waits for them, and re-layouts: 14.2 us -> 191 us
    another operation x6 -> x7, other arithmetic: 2.58 us -> 90.4 us  [the longest x1 87.3 us: _extend_modes(): arr_now = jnp.stack([*everything[::-1], here_x, *x_new], axis=0)]
  transfers between devices with their start and end apart: 6 -> 8, of which waited for: 5 -> 6; matrix products, arithmetic and copies ran while one was open for 4% -> 3% of each run, Pallas kernels for 0% -> 0%
where the time goes in v1:
time: 2440 us; the launch traced here: 2430 us
  waiting for transfers between devices  1100 us (45%)
  local copies, waits for them, and re-layouts  866 us (35%)
  other arithmetic  175 us (7%)
  matrix products  138 us (6%)
  blocking collectives  121 us (5%)
    ppermute x2, waiting for transfers between devices, _extend_modes(): ppermute(everything[-1] if everything else here_x, axis_key, buffers)  874 us
    gather x256, local copies, waits for them, and re-layouts  559 us
    unnamed x161, local copies, waits for them, and re-layouts  191 us
    all_gather x1, waiting for transfers between devices, shards(): gathered = lax.all_gather(tokens, 'heads', axis=1, tiled=True)  151 us
    all_to_all x1, blocking collectives, shards(): lax.all_to_all(ordered, 'heads', split_axis=0, concat_axis=1, tiled=True)  99.2 us
    another operation x1, other arithmetic, _extend_modes(): arr_now = jnp.stack([*everything[::-1], here_x, *x_new], axis=0)  87.3 us
    gather x1, local copies, waits for them, and re-layouts, _extend_modes(): arr_now = arr_now[(jnp.arange(n_all) - local_now) % n_all]  85 us
    dot_general x1, matrix products, shards(): jnp.dot(gathered, _extend_modes('seq', xz_weight), preferred_element_type...  80.2 us
  transfers between devices with their start and end apart: 8, of which 6 were waited for; matrix products, arithmetic and copies ran while one was open for 3% of the time, Pallas kernels for 0%

profile of v1, /device:TPU:6, one launch (start us, length us, event | category | flops | bytes accessed | tf_op | source)
XLA Modules:
  0.0 2425.5 jit_solution(13867983308899697824)
XLA Ops:
  9.0 719.8 %collective-permute-done = bf16[8192,2048]{1,0:T(8,128)(2,1)} collective-permute-done((bf16[8192,2048]{1,0:T(8,128)(2,1)}, bf16[8192,2048]{1,0:T(8,128)(2,1)}, u32[]{:S(2)}, u32[]{:S(2)}) %collective-permute-start) | collective-permute-done | bytes 33554464 | tf_op jit(solution)/shard_map/ppermute | solution.py:33
  729.0 151.2 %all-gather.5.cloned.1.call-done = bf16[512,8192]{1,0:T(8,128)(2,1)} async-done(((bf16[512,2048]{1,0:T(8,128)(2,1)}), bf16[512,8192]{1,0:T(8,128)(2,1)}) %all-gather.5.cloned.1.call-update) | async-done | bytes 8388624 | tf_op jit(solution)/shard_map/all_gather | solution.py:97
  880.2 11.0 convolution_convert_fusion.1
  907.9 27.6 %all-gather.7.cloned.1.call-done = bf16[512,2048]{1,0:T(8,128)(2,1)} async-done(((bf16[512,512]{1,0:T(8,128)(2,1)}), bf16[512,2048]{1,0:T(8,128)(2,1)}) %all-gather.7.cloned.1.call-update) | async-done | bytes 2097168 | tf_op jit(solution)/shard_map/all_gather | solution.py:107
  937.4 154.3 %collective-permute-done.1 = bf16[8192,2048]{1,0:T(8,128)(2,1)} collective-permute-done((bf16[8192,2048]{1,0:T(8,128)(2,1)}, bf16[8192,2048]{1,0:T(8,128)(2,1)}, u32[]{:S(2)}, u32[]{:S(2)}) %collective-permute-start.1) | collective-permute-done | bytes 33554464 | tf_op jit(solution)/shard_map/ppermute | solution.py:33
  1091.7 87.3 %pad_maximum_fusion = bf16[4,8192,2048]{2,1,0:T(8,128)(2,1)} fusion(bf16[1,8192,2048]{2,1,0:T(8,128)(2,1)} %bitcast.6, bf16[1,8192,2048]{2,1,0:T(8,128)(2,1)} %bitcast.210, bf16[1,8192,2048]{2,1,0:T(8,128)(2,1)} %bitcast.4, bf16[1,8192,2048]{2,1,0:T(8,128)(2,1)} %bitcast.3), kind=kLoop, calls=%fused_computation.53 | loop fusion | flops 201326592 | bytes 268435456 | tf_op jit(solution)/shard_map/stack | solution.py:37
  1179.1 85.0 %fusion.65 = (bf16[4,512,2048]{2,1,0:T(8,128)(2,1)}, bf16[4,512,2048]{2,1,0:T(8,128)(2,1)}, bf16[4,512,2048]{2,1,0:T(8,128)(2,1)}, bf16[4,512,2048]{2,1,0:T(8,12...) fusion(bf16[4,8192,2048]{2,1,0:T(8,128)(2,1)} %pad_maximum_fusion), kind=kLoop, calls=%fused_computation.213 | loop fusion | bytes 268435456 | tf_op jit(solution)/shard_map/gather | solution.py:41
  1268.1 35.2 %while.29 = (s32[]{:T(128)}, bf16[4,512,2048]{2,1,0:T(8,128)(2,1)}, s32[4,1]{0,1:T(1,128)S(1)}, bf16[4,512,2048]{1,2,0:T(8,128)(2,1)}, s32[]{:T(128)}) while((s32[]{:T(128)}, bf16[4,512,2048]{2,1,0:T(8,128)(2,1)}, s32[4,1]{0,1:T(1,128)S(1)}, bf16[4,512,2048]{1,2,0:T(8,128)(2,1)}, s32[]{:T(128)}) %tuple.303), condition=%wide.while_cond, body=%wide.while_body.sunk | while | flops 2 | bytes 12583501 | solution.py:41
  1303.3 7.1 constant_dynamic-update-slice_fusion.31
  1314.4 35.0 %while.30 = (s32[]{:T(128)}, bf16[4,512,2048]{2,1,0:T(8,128)(2,1)}, s32[4,1]{0,1:T(1,128)S(1)}, bf16[4,512,2048]{1,2,0:T(8,128)(2,1)}, s32[]{:T(128)}) while((s32[]{:T(128)}, bf16[4,512,2048]{2,1,0:T(8,128)(2,1)}, s32[4,1]{0,1:T(1,128)S(1)}, bf16[4,512,2048]{1,2,0:T(8,128)(2,1)}, s32[]{:T(128)}) %tuple.304), condition=%wide.while_cond.1, body=%wide.while_body.1.sunk | while | flops 2 | bytes 12583501 | solution.py:41
  1353.3 34.9 %while.31 = (s32[]{:T(128)}, bf16[4,512,2048]{2,1,0:T(8,128)(2,1)}, s32[4,1]{0,1:T(1,128)S(1)}, bf16[4,512,2048]{1,2,0:T(8,128)(2,1)}, s32[]{:T(128)}) while((s32[]{:T(128)}, bf16[4,512,2048]{2,1,0:T(8,128)(2,1)}, s32[4,1]{0,1:T(1,128)S(1)}, bf16[4,512,2048]{1,2,0:T(8,128)(2,1)}, s32[]{:T(128)}) %tuple.305), condition=%wide.while_cond.2, body=%wide.while_body.2.sunk | while | flops 2 | bytes 12583501 | solution.py:41
  1392.1 34.9 %while.32 = (s32[]{:T(128)}, bf16[4,512,2048]{2,1,0:T(8,128)(2,1)}, s32[4,1]{0,1:T(1,128)S(1)}, bf16[4,512,2048]{1,2,0:T(8,128)(2,1)}, s32[]{:T(128)}) while((s32[]{:T(128)}, bf16[4,512,2048]{2,1,0:T(8,128)(2,1)}, s32[4,1]{0,1:T(1,128)S(1)}, bf16[4,512,2048]{1,2,0:T(8,128)(2,1)}, s32[]{:T(128)}) %tuple.306), condition=%wide.while_cond.3, body=%wide.while_body.3.sunk | while | flops 2 | bytes 12583501 | solution.py:41
  1430.9 34.9 %while.33 = (s32[]{:T(128)}, bf16[4,512,2048]{2,1,0:T(8,128)(2,1)}, s32[4,1]{0,1:T(1,128)S(1)}, bf16[4,512,2048]{1,2,0:T(8,128)(2,1)}, s32[]{:T(128)}) while((s32[]{:T(128)}, bf16[4,512,2048]{2,1,0:T(8,128)(2,1)}, s32[4,1]{0,1:T(1,128)S(1)}, bf16[4,512,2048]{1,2,0:T(8,128)(2,1)}, s32[]{:T(128)}) %tuple.307), condition=%wide.while_cond.4, body=%wide.while_body.4.sunk | while | flops 2 | bytes 12583501 | solution.py:41
  1469.8 35.0 %while.34 = (s32[]{:T(128)}, bf16[4,512,2048]{2,1,0:T(8,128)(2,1)}, s32[4,1]{0,1:T(1,128)S(1)}, bf16[4,512,2048]{1,2,0:T(8,128)(2,1)}, s32[]{:T(128)}) while((s32[]{:T(128)}, bf16[4,512,2048]{2,1,0:T(8,128)(2,1)}, s32[4,1]{0,1:T(1,128)S(1)}, bf16[4,512,2048]{1,2,0:T(8,128)(2,1)}, s32[]{:T(128)}) %tuple.308), condition=%wide.while_cond.5, body=%wide.while_body.5.sunk | while | flops 2 | bytes 12583501 | solution.py:41
  1508.8 35.1 %while.35 = (s32[]{:T(128)}, bf16[4,512,2048]{2,1,0:T(8,128)(2,1)}, s32[4,1]{0,1:T(1,128)S(1)}, bf16[4,512,2048]{1,2,0:T(8,128)(2,1)}, s32[]{:T(128)}) while((s32[]{:T(128)}, bf16[4,512,2048]{2,1,0:T(8,128)(2,1)}, s32[4,1]{0,1:T(1,128)S(1)}, bf16[4,512,2048]{1,2,0:T(8,128)(2,1)}, s32[]{:T(128)}) %tuple.309), condition=%wide.while_cond.6, body=%wide.while_body.6.sunk | while | flops 2 | bytes 12583501 | solution.py:41
  1547.9 35.0 %while.36 = (s32[]{:T(128)}, bf16[4,512,2048]{2,1,0:T(8,128)(2,1)}, s32[4,1]{0,1:T(1,128)S(1)}, bf16[4,512,2048]{1,2,0:T(8,128)(2,1)}, s32[]{:T(128)}) while((s32[]{:T(128)}, bf16[4,512,2048]{2,1,0:T(8,128)(2,1)}, s32[4,1]{0,1:T(1,128)S(1)}, bf16[4,512,2048]{1,2,0:T(8,128)(2,1)}, s32[]{:T(128)}) %tuple.310), condition=%wide.while_cond.7, body=%wide.while_body.7.sunk | while | flops 2 | bytes 12583501 | solution.py:41
  1587.0 35.0 %while.37 = (s32[]{:T(128)}, bf16[4,512,2048]{2,1,0:T(8,128)(2,1)}, s32[4,1]{0,1:T(1,128)S(1)}, bf16[4,512,2048]{1,2,0:T(8,128)(2,1)}, s32[]{:T(128)}) while((s32[]{:T(128)}, bf16[4,512,2048]{2,1,0:T(8,128)(2,1)}, s32[4,1]{0,1:T(1,128)S(1)}, bf16[4,512,2048]{1,2,0:T(8,128)(2,1)}, s32[]{:T(128)}) %tuple.311), condition=%wide.while_cond.8, body=%wide.while_body.8.sunk | while | flops 2 | bytes 12583501 | solution.py:41
  1625.9 34.9 %while.38 = (s32[]{:T(128)}, bf16[4,512,2048]{2,1,0:T(8,128)(2,1)}, s32[4,1]{0,1:T(1,128)S(1)}, bf16[4,512,2048]{1,2,0:T(8,128)(2,1)}, s32[]{:T(128)}) while((s32[]{:T(128)}, bf16[4,512,2048]{2,1,0:T(8,128)(2,1)}, s32[4,1]{0,1:T(1,128)S(1)}, bf16[4,512,2048]{1,2,0:T(8,128)(2,1)}, s32[]{:T(128)}) %tuple.312), condition=%wide.while_cond.9, body=%wide.while_body.9.sunk | while | flops 2 | bytes 12583501 | solution.py:41
  1664.7 34.9 %while.39 = (s32[]{:T(128)}, bf16[4,512,2048]{2,1,0:T(8,128)(2,1)}, s32[4,1]{0,1:T(1,128)S(1)}, bf16[4,512,2048]{1,2,0:T(8,128)(2,1)}, s32[]{:T(128)}) while((s32[]{:T(128)}, bf16[4,512,2048]{2,1,0:T(8,128)(2,1)}, s32[4,1]{0,1:T(1,128)S(1)}, bf16[4,512,2048]{1,2,0:T(8,128)(2,1)}, s32[]{:T(128)}) %tuple.313), condition=%wide.while_cond.10, body=%wide.while_body.10.sunk | while | flops 2 | bytes 12583501 | solution.py:41
  1703.5 34.9 %while.40 = (s32[]{:T(128)}, bf16[4,512,2048]{2,1,0:T(8,128)(2,1)}, s32[4,1]{0,1:T(1,128)S(1)}, bf16[4,512,2048]{1,2,0:T(8,128)(2,1)}, s32[]{:T(128)}) while((s32[]{:T(128)}, bf16[4,512,2048]{2,1,0:T(8,128)(2,1)}, s32[4,1]{0,1:T(1,128)S(1)}, bf16[4,512,2048]{1,2,0:T(8,128)(2,1)}, s32[]{:T(128)}) %tuple.314), condition=%wide.while_cond.11, body=%wide.while_body.11.sunk | while | flops 2 | bytes 12583501 | solution.py:41
  1742.4 34.9 %while.41 = (s32[]{:T(128)}, bf16[4,512,2048]{2,1,0:T(8,128)(2,1)}, s32[4,1]{0,1:T(1,128)S(1)}, bf16[4,512,2048]{1,2,0:T(8,128)(2,1)}, s32[]{:T(128)}) while((s32[]{:T(128)}, bf16[4,512,2048]{2,1,0:T(8,128)(2,1)}, s32[4,1]{0,1:T(1,128)S(1)}, bf16[4,512,2048]{1,2,0:T(8,128)(2,1)}, s32[]{:T(128)}) %tuple.315), condition=%wide.while_cond.12, body=%wide.while_body.12.sunk | while | flops 2 | bytes 12583501 | solution.py:41
  1781.1 34.9 %while.42 = (s32[]{:T(128)}, bf16[4,512,2048]{2,1,0:T(8,128)(2,1)}, s32[4,1]{0,1:T(1,128)S(1)}, bf16[4,512,2048]{1,2,0:T(8,128)(2,1)}, s32[]{:T(128)}) while((s32[]{:T(128)}, bf16[4,512,2048]{2,1,0:T(8,128)(2,1)}, s32[4,1]{0,1:T(1,128)S(1)}, bf16[4,512,2048]{1,2,0:T(8,128)(2,1)}, s32[]{:T(128)}) %tuple.316), condition=%wide.while_cond.13, body=%wide.while_body.13.sunk | while | flops 2 | bytes 12583501 | solution.py:41
  1820.1 35.0 %while.43 = (s32[]{:T(128)}, bf16[4,512,2048]{2,1,0:T(8,128)(2,1)}, s32[4,1]{0,1:T(1,128)S(1)}, bf16[4,512,2048]{1,2,0:T(8,128)(2,1)}, s32[]{:T(128)}) while((s32[]{:T(128)}, bf16[4,512,2048]{2,1,0:T(8,128)(2,1)}, s32[4,1]{0,1:T(1,128)S(1)}, bf16[4,512,2048]{1,2,0:T(8,128)(2,1)}, s32[]{:T(128)}) %tuple.317), condition=%wide.while_cond.14, body=%wide.while_body.14.sunk | while | flops 2 | bytes 12583501 | solution.py:41
  1859.1 35.1 %while.44 = (s32[]{:T(128)}, bf16[4,512,2048]{2,1,0:T(8,128)(2,1)}, s32[4,1]{0,1:T(1,128)S(1)}, bf16[4,512,2048]{1,2,0:T(8,128)(2,1)}, s32[]{:T(128)}) while((s32[]{:T(128)}, bf16[4,512,2048]{2,1,0:T(8,128)(2,1)}, s32[4,1]{0,1:T(1,128)S(1)}, bf16[4,512,2048]{1,2,0:T(8,128)(2,1)}, s32[]{:T(128)}) %tuple.318), condition=%wide.while_cond.15, body=%wide.while_body.15.sunk | while | flops 2 | bytes 12583501 | solution.py:41
  1894.2 7.1 constant_dynamic-update-slice_fusion.30
  1901.4 7.1 constant_dynamic-update-slice_fusion.29
  1908.5 7.1 constant_dynamic-update-slice_fusion.28
  1915.6 7.1 constant_dynamic-update-slice_fusion.27
  1922.7 7.1 constant_dynamic-update-slice_fusion.26
  1929.9 7.1 constant_dynamic-update-slice_fusion.25
  1937.0 7.2 constant_dynamic-update-slice_fusion.24
  1944.2 7.2 constant_dynamic-update-slice_fusion.23
  1951.3 7.2 constant_dynamic-update-slice_fusion.22
  1958.5 7.2 constant_dynamic-update-slice_fusion.21
  1965.6 7.1 constant_dynamic-update-slice_fusion.20
  1972.8 7.1 constant_dynamic-update-slice_fusion.19
  1979.9 7.2 constant_dynamic-update-slice_fusion.18
  1987.1 7.1 constant_dynamic-update-slice_fusion.17
  2001.3 80.2 %convolution_convert_fusion = bf16[8192,512]{1,0:T(8,128)(2,1)} fusion(bf16[8192,8192]{0,1:T(8,128)(2,1)} %bitcast.8, bf16[512,8192]{1,0:T(8,128)(2,1)} %all-gather.5.cloned.1.call-done), kind=kOutput, calls=%fused_computation.60 | convolution fusion | flops 68723671040 | bytes 150994944 | tf_op jit(solution)/shard_map/dot_general | solution.py:99
  2081.5 7.6 slice_convert_fusion
  2106.7 10.9 multiply_convert_fusion.6
  2141.2 45.3 %all-gather.9.cloned.1.call-done = f32[8,32,64,128]{3,2,1,0:T(8,128)} async-done(((f32[2,32,64,128]{3,2,1,0:T(8,128)}), f32[8,32,64,128]{3,2,1,0:T(8,128)}) %all-gather.9.cloned.1.call-update) | async-done | bytes 8388624 | tf_op jit(solution)/shard_map/all_gather | solution.py:53
  2211.1 7.4 fusion.32
  2225.6 14.6 fusion.15
  2240.2 9.5 bitcast_add_fusion.1
  2255.2 99.2 %all_to_all.24 = bf16[4,64,64,128]{3,2,1,0:T(8,128)(2,1)} all-to-all(bf16[4,64,64,128]{3,2,1,0:T(8,128)(2,1)} %bitcast.212), channel_id=1, replica_groups=mesh['groups'=2,'seq'=4,'heads'=4] {'heads'}, dimensions={0} | all-to-all | bytes 8388608 | tf_op jit(solution)/shard_map/all_to_all | solution.py:230
  2359.6 17.0 psum.7
  2376.6 30.7 %fusion.12 = bf16[512,4096]{0,1:T(8,128)(2,1)} fusion(f32[256,4096]{0,1:T(8,128)} %bitcast.214, f32[256,4096]{0,1:T(8,128)} %bitcast.213, f32[512,64,64]{0,2,1:T(8,128)} %get-tuple-element.348, f32[4096]{0:T(1024)S(1)} %copy-done.41, f32[512,2]{0,1:T(2,128)S(1)} %add_rsqrt_fusion, f32[4096]{0:T(1024)S(1)} %mul.368, f32[515,4096]{0,1:T(8,128)} %copy-done.2, ...), kind=kLoop, calls=%fused_computation.75 | loop fusion | flops 52428800 | bytes 54644736 | tf_op jit(solution)/shard_map/convert_element_type | solution.py:201
  (501 shorter events, 749.0 us)
Async XLA Ops:
  7.2 888.3 %copy-start = (bf16[8192,64]{0,1:T(8,128)(2,1)S(1)}, bf16[8192,64]{0,1:T(8,128)(2,1)}, u32[]{:S(2)}) copy-start(bf16[8192,64]{0,1:T(8,128)(2,1)} %param.19) | copy-start | bytes 3145732
  7.2 873.0 %all-gather.5.cloned.1.call-start = ((), (), s32[]{:S(2)}) async-start(), calls=%async_computation.2 | async-start | bytes 10485760 | tf_op jit(solution)/shard_map/all_gather | solution.py:97
  7.2 721.6 %collective-permute-start = (bf16[8192,2048]{1,0:T(8,128)(2,1)}, bf16[8192,2048]{1,0:T(8,128)(2,1)}, u32[]{:S(2)}, u32[]{:S(2)}) collective-permute-start(bf16[8192,2048]{1,0:T(8,128)(2,1)} %param.17), channel_id=1, source_target_pairs={{0,4},{4,8},{8,12},{12,0},{1,5},{5,9},{9,13},{13,1},{2,6},{6,10},{... | collective-permute-start | bytes 100663304 | tf_op jit(solution)/shard_map/ppermute | solution.py:33
  7.3 930.1 %collective-permute-start.2 = (bf16[8192,2048]{1,0:T(8,128)(2,1)}, bf16[8192,2048]{1,0:T(8,128)(2,1)}, u32[]{:S(2)}, u32[]{:S(2)}) collective-permute-start(bf16[8192,2048]{1,0:T(8,128)(2,1)} %param.17), channel_id=1, source_target_pairs={{4,0},{8,4},{12,8},{0,12},{5,1},{9,5},{13,9},{1,13},{6,2},{10,6},{... | collective-permute-start | bytes 100663304 | tf_op jit(solution)/shard_map/ppermute | solution.py:35
  728.8 362.8 %collective-permute-start.1 = (bf16[8192,2048]{1,0:T(8,128)(2,1)}, bf16[8192,2048]{1,0:T(8,128)(2,1)}, u32[]{:S(2)}, u32[]{:S(2)}) collective-permute-start(bf16[8192,2048]{1,0:T(8,128)(2,1)} %collective-permute-done), channel_id=1, source_target_pairs={{0,4},{4,8},{8,12},{12,0},{1,5},{5,9},{9,13},{13,1},{2,6},{6,10},{... | collective-permute-start | bytes 100663304 | tf_op jit(solution)/shard_map/ppermute | solution.py:33
  728.9 162.4 %copy-start.36 = (f32[4,4096]{1,0:T(4,128)S(1)}, f32[4,4096]{1,0:T(4,128)}, u32[]{:S(2)}) copy-start(f32[4,4096]{1,0:T(4,128)} %param.23) | copy-start | bytes 196612
  728.9 163.1 %copy-start.56 = (f32[64]{0:T(128)S(1)}, f32[64]{0:T(128)}, u32[]{:S(2)}) copy-start(f32[64]{0:T(128)} %param.21) | copy-start | bytes 772
  728.9 166.5 %copy-start.53 = (f32[64]{0:T(128)S(1)}, f32[64]{0:T(128)}, u32[]{:S(2)}) copy-start(f32[64]{0:T(128)} %param.20) | copy-start | bytes 772
  728.9 206.6 %all-gather.7.cloned.1.call-start = ((), (), s32[]{:S(2)}) async-start(), calls=%async_computation.3 | async-start | bytes 2621440 | tf_op jit(solution)/shard_map/all_gather | solution.py:107
  891.2 1295.2 %all-gather.9.cloned.1.call-start = ((), (), s32[]{:S(2)}) async-start(), calls=%async_computation.4 | async-start | bytes 10485760 | tf_op jit(solution)/shard_map/all_gather | solution.py:53
  902.0 277.0 %copy-start.12 = (f32[512,64]{0,1:T(8,128)}, f32[512,64]{0,1:T(8,128)S(1)}, u32[]{:S(2)}) copy-start(f32[512,64]{0,1:T(8,128)S(1)} %compare_select_fusion) | copy-start | bytes 393220
  905.5 273.5 %copy-start.16 = (f32[256,2,32]{0,2,1:T(8,128)}, f32[256,2,32]{0,2,1:T(8,128)S(1)}, u32[]{:S(2)}) copy-start(f32[256,2,32]{0,2,1:T(8,128)S(1)} %bitcast_bitcast_fusion) | copy-start | bytes 196612
  905.6 273.4 %copy-start.19 = (f32[256,2,32]{0,2,1:T(8,128)}, f32[256,2,32]{0,2,1:T(8,128)S(1)}, u32[]{:S(2)}) copy-start(f32[256,2,32]{0,2,1:T(8,128)S(1)} %bitcast_bitcast_fusion.1) | copy-start | bytes 196612
  906.3 272.7 %copy-start.43 = (f32[2,32]{1,0:T(2,128)}, f32[2,32]{1,0:T(2,128)S(1)}, u32[]{:S(2)}) copy-start(f32[2,32]{1,0:T(2,128)S(1)} %get-tuple-element.366) | copy-start | bytes 772
  906.3 272.7 %copy-start.46 = (f32[2,32]{1,0:T(2,128)}, f32[2,32]{1,0:T(2,128)S(1)}, u32[]{:S(2)}) copy-start(f32[2,32]{1,0:T(2,128)S(1)} %get-tuple-element.364) | copy-start | bytes 772
  906.3 272.7 %copy-start.22 = (f32[256,64]{0,1:T(8,128)}, f32[256,64]{0,1:T(8,128)S(1)}, u32[]{:S(2)}) copy-start(f32[256,64]{0,1:T(8,128)S(1)} %get-tuple-element.356) | copy-start | bytes 196612
  906.4 272.7 %copy-start.24 = (f32[256,64]{0,1:T(8,128)}, f32[256,64]{0,1:T(8,128)S(1)}, u32[]{:S(2)}) copy-start(f32[256,64]{0,1:T(8,128)S(1)} %get-tuple-element.357) | copy-start | bytes 196612
  2089.0 9.2 copy-start.44
  2089.0 9.8 copy-start.47
  2096.3 5.3 collective-permute-start.3
  2106.7 11.0 copy-start.2
  2119.3 8.3 copy-start.6
  2120.2 17.6 copy-start.13
  2120.4 19.6 copy-start.11
  2120.4 7.3 copy-start.57
  2120.4 8.0 copy-start.58
  2120.4 8.8 copy-start.55
  2120.4 10.8 copy-start.35
  2120.4 10.9 copy-start.17
  2120.4 10.9 copy-start.20
  2120.8 11.9 copy-start.14
  2120.8 11.9 copy-start.15
  2186.7 9.2 copy-start.40
  2186.7 9.2 copy-start.45
  2204.2 6.9 copy-start.37
  2204.2 6.9 copy-start.39
  2211.1 7.5 copy-start.8
  2211.1 7.5 copy-start.10
  2211.1 7.5 copy-start.18
  2211.1 7.5 copy-start.23
  2211.1 7.5 copy-start.38
  2218.5 6.9 copy-start.5
  2218.5 6.9 slice-start
  2225.5 14.6 slice-start.3
  2225.6 14.6 copy-start.42
  2255.2 121.4 %copy-start.41 = (f32[4096]{0:T(1024)S(1)}, f32[4096]{0:T(1024)}, u32[]{:S(2)}) copy-start(f32[4096]{0:T(1024)} %param.27) | copy-start | bytes 49156
  2354.4 59.2 %all-to-all-start.1 = ((bf16[1,256,64,128]{3,2,0,1:T(8,128)(2,1)}), bf16[1,256,64,128]{3,2,0,1:T(8,128)(2,1)}, u32[]{:S(2)}, u32[]{:S(2)}) async-start(bf16[1,256,64,128]{3,2,0,1:T(8,128)(2,1)} %bitcast.211), calls=%async_computation.1 | async-start | bytes 8388608 | tf_op jit(solution)/shard_map/all_to_all | solution.py:229
  2376.6 42.2 %copy-start.1 = (bf16[8192,64]{0,1:T(8,128)(2,1)S(1)}, bf16[8192,64]{0,1:T(8,128)(2,1)}, u32[]{:S(2)}) copy-start(bf16[8192,64]{0,1:T(8,128)(2,1)} %param.19) | copy-start | bytes 3145732
  (24 other events, 121.1 us)
Sparse Core Ops, SparseCore 0:
  729.0 151.1 all-gather.4
  891.4 44.0 all-gather.6
  2127.8 58.5 all-gather.8
